TPU v7x, 32 devices: a whole 2x2x4 slice. The times are simulated.
32 devices in a mesh: grp: 2 (over y), patch: 8 (over z, x), frame: 2 (over core).
Axes of the slice: x: 2, y: 2, z: 4, core: 2. Of those that a mesh axis runs over, the one named last changes fastest.
Arguments:
- video_tokens: bfloat16 [4, 16, 80, 1152], P('grp', 'frame', 'patch'), parts along dimension 0, may hold values from -6 to 6
- timestep: int32 [2], P('grp'), parts along dimension 0, may hold values from 0 to 999
- w_qkv: bfloat16 [2, 1152, 1728], P(None, 'patch'), may hold values from -0.1875 to 0.1875
- w_out: bfloat16 [2, 576, 1152], P(None, None, 'patch'), may hold values from -0.25 to 0.25
- qk_gain: float32 [2, 2, 72], replicated, may hold values from 1 to 2.5
- mod_table: float32 [2, 3, 1152], replicated, may hold values from -3 to 3
- mod_gain: float32 [2, 3, 1152], replicated, may hold values from -3 to 3
Outputs:
- denoised: bfloat16 [4, 16, 80, 1152], P('grp', 'frame', 'patch'), parts along dimension 0
There are 2 independent parts, one for each index of `grp`. A program takes and returns all parts, laid end to end along the dimension named above; an argument that names none is the same for every part. Nothing has to cross between parts.
All inputs are finite; a program needn't handle non-finite values.
Results may differ from a plain program's by a relative error of at most 0.013.
Values may be sent and summed in bfloat16 or wider, within the bound.
A program may use at most 128 MiB of HBM per device.

v0:
```python
import math
import jax
import jax.numpy as jnp
from jax import lax
from jax.sharding import PartitionSpec as P


def time_embed(timestep, width):
    half_width = width // 2
    freqs = jnp.exp(-math.log(10000.0) * jnp.arange(half_width, dtype=jnp.float32) / half_width)
    angles = timestep[0].astype(jnp.float32) * freqs
    return jnp.concatenate([jnp.cos(angles), jnp.sin(angles)])


def modulate(tokens, table, gains, embed):
    params = table + gains * embed[None, :]
    values = tokens.astype(jnp.float32)
    centre = jnp.mean(values, axis=-1, keepdims=True)
    centred = values - centre
    spread = jnp.mean(centred * centred, axis=-1, keepdims=True)
    normed = centred * lax.rsqrt(spread + 1e-06)
    return ((normed * (1.0 + params[1]) + params[0]).astype(jnp.bfloat16), params[2])


def head_norm(values, gain):
    meansq = jnp.mean(values * values, axis=-1, keepdims=True)
    return (values * lax.rsqrt(meansq + 1e-06) * gain).astype(jnp.bfloat16)


def fetch_weights(qkv_rows, out_cols):
    return (
        lax.all_gather(qkv_rows, "patch", axis=0, tiled=True),
        lax.all_gather(out_cols, "patch", axis=1, tiled=True),
    )


def attend_items(stacked):
    head_size = stacked.shape[-1]
    query = stacked[0, 0]
    key = stacked[1, 0]
    value = stacked[2, 0]
    scores = jnp.einsum("nqd,nkd->nqk", query, key, preferred_element_type=jnp.float32) / math.sqrt(
        head_size
    )
    raised = jnp.exp(scores)
    total = jnp.sum(raised, axis=-1, keepdims=True)
    summed = jnp.einsum(
        "nqk,nkd->nqd", raised.astype(jnp.bfloat16), value, preferred_element_type=jnp.float32
    )
    return (summed / total).astype(jnp.bfloat16)[None]


def spatial(query, key, value, videos, fr_dev, patch_dev):
    rows, heads, head_size = query.shape
    groups = lax.axis_size("patch")
    per_group = videos * fr_dev * heads // groups
    stacked = jnp.stack([query, key, value])
    stacked = stacked.reshape(3, videos * fr_dev, patch_dev, heads, head_size)
    stacked = stacked.transpose(0, 1, 3, 2, 4).reshape(3, groups, per_group, patch_dev, head_size)
    attended = attend_items(
        lax.all_to_all(stacked, "patch", split_axis=1, concat_axis=3, tiled=True)
    )
    returned = lax.all_to_all(attended, "patch", split_axis=2, concat_axis=0, tiled=True)
    returned = returned.reshape(videos * fr_dev, heads, patch_dev, head_size).transpose(0, 2, 1, 3)
    return returned.reshape(rows, heads * head_size)


def frame_attend(query, key, value, heads):
    videos, q_frames, patches, feat = query.shape
    k_frames = key.shape[1]
    head_size = feat // heads
    query = query.reshape(videos, q_frames, patches, heads, head_size)
    key = key.reshape(videos, k_frames, patches, heads, head_size)
    value = value.reshape(videos, k_frames, patches, heads, head_size)
    scores = jnp.einsum(
        "bfphd,bgphd->bphfg", query, key, preferred_element_type=jnp.float32
    ) / math.sqrt(head_size)
    raised = jnp.exp(scores)
    total = jnp.sum(raised, axis=-1)
    summed = jnp.einsum(
        "bphfg,bgphd->bfphd", raised.astype(jnp.bfloat16), value, preferred_element_type=jnp.float32
    )
    result = summed / total.transpose(0, 3, 1, 2)[..., None]
    return result.astype(jnp.bfloat16).reshape(videos, q_frames, patches, feat)


def temporal(query, key, value, videos, fr_dev, patch_dev):
    rows, heads, head_size = query.shape
    feat = heads * head_size
    query4 = query.reshape(videos, fr_dev, patch_dev, feat)
    key4 = key.reshape(videos, fr_dev, patch_dev, feat)
    value4 = value.reshape(videos, fr_dev, patch_dev, feat)
    joined = jnp.concatenate([query4, key4, value4], axis=3)
    swapped = lax.all_to_all(joined, "frame", split_axis=2, concat_axis=1, tiled=True)
    result = frame_attend(
        swapped[..., :feat], swapped[..., feat : 2 * feat], swapped[..., 2 * feat :], heads
    )
    returned = lax.all_to_all(result, "frame", split_axis=1, concat_axis=2, tiled=True)
    return returned.reshape(rows, feat)


def per_device(video_tokens, timestep, w_qkv, w_out, qk_gain, mod_table, mod_gain):
    videos, fr_dev, patch_dev, width = video_tokens.shape
    rows = videos * fr_dev * patch_dev
    head_size = qk_gain.shape[2]
    heads = w_out.shape[1] // head_size
    embed = time_embed(timestep, width)
    tokens = video_tokens.reshape(rows, width)
    for layer in range(2):
        qkv_full, out_full = fetch_weights(w_qkv[layer], w_out[layer])
        mixed, gate = modulate(tokens, mod_table[layer], mod_gain[layer], embed)
        joint = jnp.dot(mixed, qkv_full, preferred_element_type=jnp.float32)
        joint = joint.reshape(rows, 3, heads, head_size)
        query = head_norm(joint[:, 0], qk_gain[layer, 0])
        key = head_norm(joint[:, 1], qk_gain[layer, 1])
        value = joint[:, 2].astype(jnp.bfloat16)
        if layer == 0:
            attended = spatial(query, key, value, videos, fr_dev, patch_dev)
        else:
            attended = temporal(query, key, value, videos, fr_dev, patch_dev)
        update = jnp.dot(attended, out_full, preferred_element_type=jnp.float32)
        tokens = (tokens.astype(jnp.float32) + gate * update).astype(jnp.bfloat16)
    return tokens.reshape(videos, fr_dev, patch_dev, width)


def solution(mesh):
    placed = (
        P("grp", "frame", "patch", None),
        P("grp"),
        P(None, "patch", None),
        P(None, None, "patch"),
        P(),
        P(),
        P(),
    )
    return jax.shard_map(
        per_device,
        mesh=mesh,
        in_specs=placed,
        out_specs=P("grp", "frame", "patch", None),
        check_vma=False,
    )
```

profile of v0, /device:TPU:0, one launch (start us, length us, event | category | flops | bytes accessed | tf_op | source)
XLA Modules:
  0.0 268.2 jit_solution(7167278873392558477)
XLA Ops:
  6.6 2.3 fusion.36
  9.0 0.8 fusion.39
  9.8 0.7 all-gather.13.cloned.1.call-update
  12.4 72.5 %all-gather.9.cloned.1.call-done = bf16[1,1152,1728]{2,1,0:T(8,128)(2,1)} async-done(((bf16[1,144,1728]{2,1,0:T(8,128)(2,1)}), bf16[1,1152,1728]{2,1,0:T(8,128)(2,1)}) %all-gather.9.cloned.1.call-update) | async-done | bytes 3981328 | tf_op jit(solution)/shard_map/all_gather | solution.py:32
  84.8 6.5 %copy.88 = bf16[1728,1152]{1,0:T(8,128)(2,1)} copy(bf16[1728,1152]{0,1:T(8,128)(2,1)} %bitcast.115) | data formatting | bytes 7962624 | tf_op jit(solution)/shard_map/dot_general | solution.py:112
  91.4 3.6 %fusion.15 = f32[160,3,8,72]{0,3,2,1:T(8,128)S(1)} fusion(bf16[3,8,72,1152]{3,2,1,0:T(8,128)(2,1)} %bitcast.116, bf16[160,1152,1,1]{1,0,2,3:T(8,128)(2,1)S(1)} %reshape.231), kind=kOutput, calls=%fused_computation.38 | convolution fusion | flops 637009920 | bytes 5455872 | tf_op jit(solution)/shard_map/dot_general | solution.py:112
  97.8 40.4 %all_to_all.63 = bf16[3,8,16,10,72]{4,2,3,0,1:T(8,128)(2,1)S(1)} all-to-all(bf16[3,8,16,10,72]{4,2,3,0,1:T(8,128)(2,1)S(1)} %copy.95), channel_id=1, replica_groups=mesh['grp'=2,'patch'=8,'frame'=2] {'patch'}, dimensions={1} | all-to-all | bytes 1105920 | tf_op jit(solution)/shard_map/all_to_all | solution.py:61
  138.3 0.3 fusion.42
  138.7 0.4 fusion.14
  139.1 1.0 copy.100
  140.1 3.7 %all-to-all-start.1 = ((bf16[1,16,80,72]{3,1,0,2:T(8,128)(2,1)}), bf16[1,16,80,72]{3,1,0,2:T(8,128)(2,1)S(1)}, u32[]{:S(2)}, u32[]{:S(2)}) async-start(bf16[1,16,80,72]{3,1,0,2:T(8,128)(2,1)} %copy.100), calls=%async_computation.1 | async-start | bytes 655360 | tf_op jit(solution)/shard_map/all_to_all | solution.py:63
  144.0 0.3 all-gather.15.cloned.1.call-update
  144.7 15.2 %all-to-all-done.1 = bf16[1,16,80,72]{3,1,0,2:T(8,128)(2,1)S(1)} async-done(((bf16[1,16,80,72]{3,1,0,2:T(8,128)(2,1)}), bf16[1,16,80,72]{3,1,0,2:T(8,128)(2,1)S(1)}, u32[]{:S(2)}, u32[]{:S(2)}) %all-to-all-start.1) | async-done | bytes 184352 | tf_op jit(solution)/shard_map/all_to_all | solution.py:63
  160.3 2.1 fusion.43
  162.6 52.2 %all-gather.13.cloned.1.call-done = bf16[1,1152,1728]{2,1,0:T(8,128)(2,1)} async-done(((bf16[1,144,1728]{2,1,0:T(8,128)(2,1)}), bf16[1,1152,1728]{2,1,0:T(8,128)(2,1)}) %all-gather.13.cloned.1.call-update) | async-done | bytes 3981328 | tf_op jit(solution)/shard_map/all_gather | solution.py:32
  214.8 4.2 %fusion = f32[160,1728]{1,0:T(8,128)} fusion(bf16[1,1152,1728]{2,1,0:T(8,128)(2,1)} %all-gather.13.cloned.1.call-done, f32[160,1152]{1,0:T(8,128)S(1)} %get-tuple-element.42, f32[1152]{0:T(1024)S(1)} %get-tuple-element.10, f32[1152]{0:T(1024)S(1)} %get-tuple-element.11, f32[160]{0:T(256)S(1)} %add_rsqrt_fusion.5, f32[160]{0:T(256)S(1)} %broadcast_multiply_fusion.1), kind=kOutput, calls=%fused_computation | convolution fusion | flops 637931520 | bytes 5835008 | tf_op jit(solution)/shard_map/dot_general | solution.py:112
  219.0 2.2 reshape.219
  221.2 0.8 slice.163
  222.0 1.1 multiply_reduce_fusion.2
  224.9 1.4 squeeze.62
  226.2 2.1 convert_element_type.113
  228.3 0.8 multiply_convert_fusion
  229.1 0.8 multiply_convert_fusion.1
  230.1 1.4 concatenate.8
  231.6 4.2 %all_to_all.64 = bf16[2,8,10,1728]{3,1,0,2:T(8,128)(2,1)S(1)} all-to-all(bf16[2,8,10,1728]{3,1,0,2:T(8,128)(2,1)S(1)} %copy.108), channel_id=1, replica_groups=mesh['grp'=2,'patch'=8,'frame'=2] {'frame'}, dimensions={2} | all-to-all | bytes 1105920 | tf_op jit(solution)/shard_map/all_to_all | solution.py:94
  237.0 0.4 fusion.44
  237.4 0.4 fusion.12
  237.9 0.6 reshape.233
  238.5 3.9 %all_to_all.65 = bf16[2,16,5,576]{3,0,2,1:T(2,128)(2,1)S(1)} all-to-all(bf16[2,16,5,576]{3,0,2,1:T(2,128)(2,1)S(1)} %reshape.233), channel_id=1, replica_groups=mesh['grp'=2,'patch'=8,'frame'=2] {'frame'}, dimensions={1} | all-to-all | bytes 368640 | tf_op jit(solution)/shard_map/all_to_all | solution.py:98
  242.5 16.2 %all-gather.15.cloned.1.call-done = bf16[1,576,1152]{1,2,0:T(8,128)(2,1)} async-done(((bf16[1,576,144]{1,2,0:T(8,128)(2,1)}), bf16[1,576,1152]{1,2,0:T(8,128)(2,1)}) %all-gather.15.cloned.1.call-update) | async-done | bytes 1327120 | tf_op jit(solution)/shard_map/all_gather | solution.py:33
  258.8 2.0 fusion.6
  260.9 0.8 copy.118
  (83 shorter events, 9.0 us)
Async XLA Ops:
  6.5 2.4 copy-start.2
  6.5 4.8 %copy-start.4 = (f32[2,3,1152]{2,0,1:T(2,128)S(1)}, f32[2,3,1152]{2,0,1:T(2,128)}, u32[]{:S(2)}) copy-start(f32[2,3,1152]{2,0,1:T(2,128)} %param.12) | copy-start | bytes 82948
  6.5 4.8 %copy-start.3 = (f32[2,3,1152]{2,0,1:T(2,128)S(1)}, f32[2,3,1152]{2,0,1:T(2,128)}, u32[]{:S(2)}) copy-start(f32[2,3,1152]{2,0,1:T(2,128)} %param.13) | copy-start | bytes 82948
  6.5 4.9 %copy-start = (bf16[2,8,10,1152]{3,1,2,0:T(8,128)(2,1)S(1)}, bf16[2,8,10,1152]{3,1,2,0:T(8,128)(2,1)}, u32[]{:S(2)}) copy-start(bf16[2,8,10,1152]{3,1,2,0:T(8,128)(2,1)} %param.7) | copy-start | bytes 1105924
  6.5 78.3 %all-gather.9.cloned.1.call-start = ((), (), s32[]{:S(2)}) async-start(), calls=%async_computation.4 | async-start | bytes 4644864 | tf_op jit(solution)/shard_map/all_gather | solution.py:32
  8.9 151.4 %all-gather.11.cloned.1.call-start = ((), (), s32[]{:S(2)}) async-start(), calls=%async_computation.5 | async-start | bytes 1658880 | tf_op jit(solution)/shard_map/all_gather | solution.py:33
  9.8 205.1 %all-gather.13.cloned.1.call-start = ((), (), s32[]{:S(2)}) async-start(), calls=%async_computation.6 | async-start | bytes 4644864 | tf_op jit(solution)/shard_map/all_gather | solution.py:32
  11.4 0.9 copy-start.5
  140.1 19.9 %all-to-all-start.1 = ((bf16[1,16,80,72]{3,1,0,2:T(8,128)(2,1)}), bf16[1,16,80,72]{3,1,0,2:T(8,128)(2,1)S(1)}, u32[]{:S(2)}, u32[]{:S(2)}) async-start(bf16[1,16,80,72]{3,1,0,2:T(8,128)(2,1)} %copy.100), calls=%async_computation.1 | async-start | bytes 655360 | tf_op jit(solution)/shard_map/all_to_all | solution.py:63
  143.7 115.0 %all-gather.15.cloned.1.call-start = ((), (), s32[]{:S(2)}) async-start(), calls=%async_computation.7 | async-start | bytes 1658880 | tf_op jit(solution)/shard_map/all_gather | solution.py:33
  229.1 1.0 copy-start.1
Sparse Core Ops, SparseCore 0:
  9.6 75.2 all-gather.8
  87.0 51.2 all-gather.10
  140.5 74.2 all-gather.12
  216.9 41.8 all-gather.14
where the time goes:
time: 269 us; the launch traced here: 268 us
  waiting for transfers between devices  157 us (58%)
  blocking collectives  48.4 us (18%)
  local copies, waits for them, and re-layouts  26.3 us (10%)
  between operations  14.2 us (5%)
  matrix products  13.3 us (5%)
  other arithmetic  4.76 us (2%)
  starting transfers between devices  4 us (1%)
    all_gather x2, waiting for transfers between devices, fetch_weights(): lax.all_gather(qkv_rows, 'patch', axis=0, tiled=True)  125 us
    all_to_all x1, blocking collectives, spatial(): lax.all_to_all(stacked, 'patch', split_axis=1, concat_axis=3, tiled=True)  40.4 us
    all_gather x2, waiting for transfers between devices, fetch_weights(): lax.all_gather(out_cols, 'patch', axis=1, tiled=True)  16.3 us
    all_to_all x1, waiting for transfers between devices, spatial(): lax.all_to_all(attended, 'patch', split_axis=2, concat_axis=0, tiled=True)  15.2 us
    dot_general x2, matrix products, per_device(): joint = jnp.dot(mixed, qkv_full, preferred_element_type=jnp.float32)  7.8 us
    dot_general x1, local copies, waits for them, and re-layouts, per_device(): joint = jnp.dot(mixed, qkv_full, preferred_element_type=jnp.float32)  6.5 us
  transfers between devices with their start and end apart: 5, of which 4 were waited for; matrix products, arithmetic and copies ran while one was open for 15% of the time, Pallas kernels for 0%

commit v1 on v0

--- a/solution.py
+++ b/solution.py
@@ -1,8 +1,31 @@
+import functools
 import math
 import jax
 import jax.numpy as jnp
 from jax import lax
 from jax.sharding import PartitionSpec as P
+
+
+def convert_the_row(z_in, peer_axis):
+    copies = []
+    local_now, ready, q_next = (lax.psum(1, peer_axis), lax.axis_index(peer_axis), z_in.shape[1])
+    for hop_no, p in enumerate(z_in.shape):
+        copies.append(p * local_now if hop_no == 1 else p)
+    earlier = lax.dynamic_update_slice_in_dim(
+        jnp.zeros(copies, z_in.dtype), z_in, ready * q_next, axis=1
+    )
+    for at in tuple(range(1, local_now)):
+        found = []
+        for hop_no in tuple(range(local_now)):
+            found.append((hop_no, (hop_no + 1) % local_now))
+        z_in = lax.ppermute(z_in, peer_axis, found)
+        earlier = lax.dynamic_update_slice_in_dim(
+            earlier, z_in, (ready - at) % local_now * q_next, axis=1
+        )
+    return earlier
+
+
+task_search = functools.partial(convert_the_row, peer_axis="patch")
 
 
 def time_embed(timestep, width):
@@ -28,10 +51,7 @@
 
 
 def fetch_weights(qkv_rows, out_cols):
-    return (
-        lax.all_gather(qkv_rows, "patch", axis=0, tiled=True),
-        lax.all_gather(out_cols, "patch", axis=1, tiled=True),
-    )
+    return (lax.all_gather(qkv_rows, "patch", axis=0, tiled=True), task_search(out_cols))
 
 
 def attend_items(stacked):

time: 269 us -> 264 us (0.981)
  blocking collectives: 48.4 us -> 8.05 us
  starting transfers between devices: 4 us -> 31.1 us
  local copies, waits for them, and re-layouts: 26.3 us -> 44.8 us
  waiting for transfers between devices: 157 us -> 146 us
  other arithmetic: 4.76 us -> 7.68 us
  matrix products: 13.3 us -> 10.6 us
    ppermute x0 -> x14, waiting for transfers between devices: none -> 72.6 us  [convert_the_row(): z_in = lax.ppermute(z_in, peer_axis, found)]
    all_gather x2, waiting for transfers between devices: 125 us -> 66.3 us  [fetch_weights(): lax.all_gather(qkv_rows, 'patch', axis=0, tiled=True)]
    all_to_all x1 -> x0, blocking collectives: 40.4 us -> none  [spatial(): lax.all_to_all(stacked, 'patch', split_axis=1, concat_axis=3, tiled=True)]
    ppermute x0 -> x14, starting transfers between devices: none -> 22.8 us  [convert_the_row(): z_in = lax.ppermute(z_in, peer_axis, found)]
    all_gather x2 -> x0, waiting for transfers between devices: 16.3 us -> none  [fetch_weights(): lax.all_gather(out_cols, 'patch', axis=1, tiled=True)]
    dynamic_update_slice x0 -> x15, local copies, waits for them, and re-layouts: none -> 9.74 us  [the longest x13 9.68 us: convert_the_row(): lax.dynamic_update_slice_in_dim(earlier, z_in, (ready - at) % local_now *...]
    all_to_all x1, waiting for transfers between devices: 15.2 us -> 7.27 us  [spatial(): lax.all_to_all(attended, 'patch', split_axis=2, concat_axis=0, tiled=True)]
    all_to_all x0 -> x1, starting transfers between devices: none -> 3.55 us  [spatial(): lax.all_to_all(stacked, 'patch', split_axis=1, concat_axis=3, tiled=True)]
  transfers between devices with their start and end apart: 5 -> 18, of which waited for: 4 -> 12; matrix products, arithmetic and copies ran while one was open for 15% -> 13% of each run, Pallas kernels for 0% -> 0%
where the time goes in v1:
time: 264 us; the launch traced here: 263 us
  waiting for transfers between devices  146 us (55%)
  local copies, waits for them, and re-layouts  44.8 us (17%)
  starting transfers between devices  31.1 us (12%)
  between operations  14.7 us (6%)
  matrix products  10.6 us (4%)
  blocking collectives  8.05 us (3%)
  other arithmetic  7.68 us (3%)
    ppermute x14, waiting for transfers between devices, convert_the_row(): z_in = lax.ppermute(z_in, peer_axis, found)  72.6 us
    all_gather x2, waiting for transfers between devices, fetch_weights(): lax.all_gather(qkv_rows, 'patch', axis=0, tiled=True)  66.3 us
    ppermute x14, starting transfers between devices, convert_the_row(): z_in = lax.ppermute(z_in, peer_axis, found)  22.8 us
    dynamic_update_slice x13, local copies, waits for them, and re-layouts, convert_the_row(): lax.dynamic_update_slice_in_dim(earlier, z_in, (ready - at) % local_now *...  9.68 us
    dot_general x2, matrix products, per_device(): joint = jnp.dot(mixed, qkv_full, preferred_element_type=jnp.float32)  7.92 us
    all_to_all x1, waiting for transfers between devices, spatial(): lax.all_to_all(attended, 'patch', split_axis=2, concat_axis=0, tiled=True)  7.27 us
    dot_general x1, local copies, waits for them, and re-layouts, per_device(): joint = jnp.dot(mixed, qkv_full, preferred_element_type=jnp.float32)  6.46 us
  transfers between devices with their start and end apart: 18, of which 12 were waited for; matrix products, arithmetic and copies ran while one was open for 13% of the time, Pallas kernels for 0%

profile of v1, /device:TPU:0, one launch (start us, length us, event | category | flops | bytes accessed | tf_op | source)
XLA Modules:
  0.0 263.2 jit_solution(6337880620391389853)
XLA Ops:
  6.5 2.3 fusion.34
  9.8 2.9 %collective-permute-start.7 = (bf16[576,144]{0,1:T(8,128)(2,1)}, bf16[576,144]{0,1:T(8,128)(2,1)}, u32[]{:S(2)}, u32[]{:S(2)}) collective-permute-start(bf16[576,144]{0,1:T(8,128)(2,1)} %get-tuple-element.27), channel_id=1, source_target_pairs={{0,2},{2,4},{4,6},{6,8},{8,10},{10,12},{12,14},{14,0},{1,3},{3,5},... | collective-permute-start | bytes 497672 | tf_op jit(solution)/shard_map/ppermute | solution.py:21
  12.7 1.5 collective-permute-start
  22.2 2.5 collective-permute-done
  24.8 1.6 constant_dynamic-update-slice_fusion.6
  26.4 66.3 %all-gather.5.cloned.1.call-done = bf16[1,1152,1728]{2,1,0:T(8,128)(2,1)} async-done(((bf16[1,144,1728]{2,1,0:T(8,128)(2,1)}), bf16[1,1152,1728]{2,1,0:T(8,128)(2,1)}) %all-gather.5.cloned.1.call-update) | async-done | bytes 3981328 | tf_op jit(solution)/shard_map/all_gather | solution.py:54
  92.7 6.5 %copy.88 = bf16[1728,1152]{1,0:T(8,128)(2,1)} copy(bf16[1728,1152]{0,1:T(8,128)(2,1)} %bitcast.117) | data formatting | bytes 7962624 | tf_op jit(solution)/shard_map/dot_general | solution.py:132
  99.1 3.7 %fusion.13 = f32[160,3,8,72]{0,3,2,1:T(8,128)S(1)} fusion(bf16[3,8,72,1152]{3,2,1,0:T(8,128)(2,1)} %bitcast.118, bf16[160,1152,1,1]{1,0,2,3:T(8,128)(2,1)S(1)} %reshape.229), kind=kOutput, calls=%fused_computation.36 | convolution fusion | flops 637009920 | bytes 5455872 | tf_op jit(solution)/shard_map/dot_general | solution.py:132
  111.4 3.6 %all-to-all-start = ((bf16[3,8,16,10,72]{4,2,3,0,1:T(8,128)(2,1)}), bf16[3,8,16,10,72]{4,2,3,0,1:T(8,128)(2,1)S(1)}, u32[]{:S(2)}, u32[]{:S(2)}) async-start(bf16[3,8,16,10,72]{4,2,3,0,1:T(8,128)(2,1)} %copy.95), calls=%async_computation | async-start | bytes 1966080 | tf_op jit(solution)/shard_map/all_to_all | solution.py:81
  115.9 2.0 collective-permute-start.9
  119.4 1.6 constant_dynamic-update-slice_fusion.5
  121.9 27.6 %collective-permute-done.9 = bf16[576,144]{0,1:T(8,128)(2,1)S(1)} collective-permute-done((bf16[576,144]{0,1:T(8,128)(2,1)}, bf16[576,144]{0,1:T(8,128)(2,1)S(1)}, u32[]{:S(2)}, u32[]{:S(2)}) %collective-permute-start.9) | collective-permute-done | bytes 165920 | tf_op jit(solution)/shard_map/ppermute | solution.py:21
  149.5 7.9 %collective-permute-done.2 = bf16[576,144]{0,1:T(8,128)(2,1)S(1)} collective-permute-done((bf16[576,144]{0,1:T(8,128)(2,1)}, bf16[576,144]{0,1:T(8,128)(2,1)S(1)}, u32[]{:S(2)}, u32[]{:S(2)}) %collective-permute-start.2) | collective-permute-done | bytes 165920 | tf_op jit(solution)/shard_map/ppermute | solution.py:21
  158.1 7.2 %collective-permute-done.10 = bf16[576,144]{0,1:T(8,128)(2,1)S(1)} collective-permute-done((bf16[576,144]{0,1:T(8,128)(2,1)S(1)}, bf16[576,144]{0,1:T(8,128)(2,1)S(1)}, u32[]{:S(2)}, u32[]{:S(2)}) %collective-permute-start.10) | collective-permute-done | bytes 165920 | tf_op jit(solution)/shard_map/ppermute | solution.py:21
  165.5 7.7 %collective-permute-done.3 = bf16[576,144]{0,1:T(8,128)(2,1)S(1)} collective-permute-done((bf16[576,144]{0,1:T(8,128)(2,1)S(1)}, bf16[576,144]{0,1:T(8,128)(2,1)S(1)}, u32[]{:S(2)}, u32[]{:S(2)}) %collective-permute-start.3) | collective-permute-done | bytes 165920 | tf_op jit(solution)/shard_map/ppermute | solution.py:21
  173.2 2.9 %collective-permute-start.4 = (bf16[576,144]{0,1:T(8,128)(2,1)S(1)}, bf16[576,144]{0,1:T(8,128)(2,1)S(1)}, u32[]{:S(2)}, u32[]{:S(2)}) collective-permute-start(bf16[576,144]{0,1:T(8,128)(2,1)S(1)} %collective-permute-done.3), channel_id=1, source_target_pairs={{0,2},{2,4},{4,6},{6,8},{8,10},{10,12},{12,14},{14,0},{1,3},{3,5},... | collective-permute-start | bytes 497672 | tf_op jit(solution)/shard_map/ppermute | solution.py:21
  176.9 4.3 %collective-permute-done.11 = bf16[576,144]{0,1:T(8,128)(2,1)S(1)} collective-permute-done((bf16[576,144]{0,1:T(8,128)(2,1)S(1)}, bf16[576,144]{0,1:T(8,128)(2,1)S(1)}, u32[]{:S(2)}, u32[]{:S(2)}) %collective-permute-start.11) | collective-permute-done | bytes 165920 | tf_op jit(solution)/shard_map/ppermute | solution.py:21
  181.2 2.9 %collective-permute-start.12 = (bf16[576,144]{0,1:T(8,128)(2,1)S(1)}, bf16[576,144]{0,1:T(8,128)(2,1)S(1)}, u32[]{:S(2)}, u32[]{:S(2)}) collective-permute-start(bf16[576,144]{0,1:T(8,128)(2,1)S(1)} %collective-permute-done.11), channel_id=1, source_target_pairs={{0,2},{2,4},{4,6},{6,8},{8,10},{10,12},{12,14},{14,0},{1,3},{3,5},... | collective-permute-start | bytes 497672 | tf_op jit(solution)/shard_map/ppermute | solution.py:21
  184.1 4.9 %collective-permute-done.4 = bf16[576,144]{0,1:T(8,128)(2,1)S(1)} collective-permute-done((bf16[576,144]{0,1:T(8,128)(2,1)S(1)}, bf16[576,144]{0,1:T(8,128)(2,1)S(1)}, u32[]{:S(2)}, u32[]{:S(2)}) %collective-permute-start.4) | collective-permute-done | bytes 165920 | tf_op jit(solution)/shard_map/ppermute | solution.py:21
  189.0 2.8 %collective-permute-start.5 = (bf16[576,144]{0,1:T(8,128)(2,1)S(1)}, bf16[576,144]{0,1:T(8,128)(2,1)S(1)}, u32[]{:S(2)}, u32[]{:S(2)}) collective-permute-start(bf16[576,144]{0,1:T(8,128)(2,1)S(1)} %collective-permute-done.4), channel_id=1, source_target_pairs={{0,2},{2,4},{4,6},{6,8},{8,10},{10,12},{12,14},{14,0},{1,3},{3,5},... | collective-permute-start | bytes 497672 | tf_op jit(solution)/shard_map/ppermute | solution.py:21
  192.5 4.4 %collective-permute-done.12 = bf16[576,144]{0,1:T(8,128)(2,1)S(1)} collective-permute-done((bf16[576,144]{0,1:T(8,128)(2,1)S(1)}, bf16[576,144]{0,1:T(8,128)(2,1)S(1)}, u32[]{:S(2)}, u32[]{:S(2)}) %collective-permute-start.12) | collective-permute-done | bytes 165920 | tf_op jit(solution)/shard_map/ppermute | solution.py:21
  196.9 2.8 %collective-permute-start.13 = (bf16[576,144]{0,1:T(8,128)(2,1)S(1)}, bf16[576,144]{0,1:T(8,128)(2,1)S(1)}, u32[]{:S(2)}, u32[]{:S(2)}) collective-permute-start(bf16[576,144]{0,1:T(8,128)(2,1)S(1)} %collective-permute-done.12), channel_id=1, source_target_pairs={{0,2},{2,4},{4,6},{6,8},{8,10},{10,12},{12,14},{14,0},{1,3},{3,5},... | collective-permute-start | bytes 497672 | tf_op jit(solution)/shard_map/ppermute | solution.py:21
  199.7 5.1 %collective-permute-done.5 = bf16[576,144]{0,1:T(8,128)(2,1)S(1)} collective-permute-done((bf16[576,144]{0,1:T(8,128)(2,1)S(1)}, bf16[576,144]{0,1:T(8,128)(2,1)S(1)}, u32[]{:S(2)}, u32[]{:S(2)}) %collective-permute-start.5) | collective-permute-done | bytes 165920 | tf_op jit(solution)/shard_map/ppermute | solution.py:21
  204.8 2.7 %collective-permute-start.6 = (bf16[576,144]{0,1:T(8,128)(2,1)S(1)}, bf16[576,144]{0,1:T(8,128)(2,1)}, u32[]{:S(2)}, u32[]{:S(2)}) collective-permute-start(bf16[576,144]{0,1:T(8,128)(2,1)S(1)} %collective-permute-done.5), channel_id=1, source_target_pairs={{0,2},{2,4},{4,6},{6,8},{8,10},{10,12},{12,14},{14,0},{1,3},{3,5},... | collective-permute-start | bytes 497672 | tf_op jit(solution)/shard_map/ppermute | solution.py:21
  209.4 4.6 %all-to-all-start.1 = ((bf16[1,16,80,72]{3,1,0,2:T(8,128)(2,1)}), bf16[1,16,80,72]{3,1,0,2:T(8,128)(2,1)S(1)}, u32[]{:S(2)}, u32[]{:S(2)}) async-start(bf16[1,16,80,72]{3,1,0,2:T(8,128)(2,1)} %copy.100), calls=%async_computation.1 | async-start | bytes 655360 | tf_op jit(solution)/shard_map/all_to_all | solution.py:83
  214.8 1.7 constant_dynamic-update-slice_fusion
  216.5 7.3 %all-to-all-done.1 = bf16[1,16,80,72]{3,1,0,2:T(8,128)(2,1)S(1)} async-done(((bf16[1,16,80,72]{3,1,0,2:T(8,128)(2,1)}), bf16[1,16,80,72]{3,1,0,2:T(8,128)(2,1)S(1)}, u32[]{:S(2)}, u32[]{:S(2)}) %all-to-all-start.1) | async-done | bytes 184352 | tf_op jit(solution)/shard_map/all_to_all | solution.py:83
  225.1 4.2 %fusion = f32[160,1728]{1,0:T(8,128)} fusion(bf16[1,1152,1728]{2,1,0:T(8,128)(2,1)} %all-gather.7.cloned.1.call-done, f32[160,1152]{1,0:T(8,128)S(1)} %get-tuple-element.42, f32[1152]{0:T(1024)S(1)} %get-tuple-element.10, f32[1152]{0:T(1024)S(1)} %get-tuple-element.11, f32[160]{0:T(256)S(1)} %add_rsqrt_fusion.5, f32[160]{0:T(256)S(1)} %broadcast_multiply_fusion.1), kind=kOutput, calls=%fused_computation | convolution fusion | flops 637931520 | bytes 5835008 | tf_op jit(solution)/shard_map/dot_general | solution.py:132
  229.2 2.2 reshape.219
  238.4 2.1 convert_element_type.113
  243.9 4.2 %all_to_all.63 = bf16[2,8,10,1728]{3,1,0,2:T(8,128)(2,1)S(1)} all-to-all(bf16[2,8,10,1728]{3,1,0,2:T(8,128)(2,1)S(1)} %copy.108), channel_id=1, replica_groups=mesh['grp'=2,'patch'=8,'frame'=2] {'frame'}, dimensions={2} | all-to-all | bytes 1105920 | tf_op jit(solution)/shard_map/all_to_all | solution.py:114
  250.8 3.9 %all_to_all.64 = bf16[2,16,5,576]{3,0,2,1:T(2,128)(2,1)S(1)} all-to-all(bf16[2,16,5,576]{3,0,2,1:T(2,128)(2,1)S(1)} %reshape.231), channel_id=1, replica_groups=mesh['grp'=2,'patch'=8,'frame'=2] {'frame'}, dimensions={1} | all-to-all | bytes 368640 | tf_op jit(solution)/shard_map/all_to_all | solution.py:118
  (135 shorter events, 40.5 us)
Async XLA Ops:
  6.5 2.4 copy-start.4
  6.5 8.5 %copy-start.9 = (f32[2,3,1152]{2,0,1:T(2,128)S(1)}, f32[2,3,1152]{2,0,1:T(2,128)}, u32[]{:S(2)}) copy-start(f32[2,3,1152]{2,0,1:T(2,128)} %param.13) | copy-start | bytes 82948
  6.5 8.5 %copy-start.10 = (f32[2,3,1152]{2,0,1:T(2,128)S(1)}, f32[2,3,1152]{2,0,1:T(2,128)}, u32[]{:S(2)}) copy-start(f32[2,3,1152]{2,0,1:T(2,128)} %param.12) | copy-start | bytes 82948
  6.5 86.1 %all-gather.5.cloned.1.call-start = ((), (), s32[]{:S(2)}) async-start(), calls=%async_computation.4 | async-start | bytes 4644864 | tf_op jit(solution)/shard_map/all_gather | solution.py:54
  8.9 6.4 %copy-start.2 = (bf16[2,8,10,1152]{3,1,2,0:T(8,128)(2,1)S(1)}, bf16[2,8,10,1152]{3,1,2,0:T(8,128)(2,1)}, u32[]{:S(2)}) copy-start(bf16[2,8,10,1152]{3,1,2,0:T(8,128)(2,1)} %param.7) | copy-start | bytes 1105924
  8.9 216.1 %all-gather.7.cloned.1.call-start = ((), (), s32[]{:S(2)}) async-start(), calls=%async_computation.5 | async-start | bytes 4644864 | tf_op jit(solution)/shard_map/all_gather | solution.py:54
  9.8 11.8 %collective-permute-start.7 = (bf16[576,144]{0,1:T(8,128)(2,1)}, bf16[576,144]{0,1:T(8,128)(2,1)}, u32[]{:S(2)}, u32[]{:S(2)}) collective-permute-start(bf16[576,144]{0,1:T(8,128)(2,1)} %get-tuple-element.27), channel_id=1, source_target_pairs={{0,2},{2,4},{4,6},{6,8},{8,10},{10,12},{12,14},{14,0},{1,3},{3,5},... | collective-permute-start | bytes 497672 | tf_op jit(solution)/shard_map/ppermute | solution.py:21
  12.7 12.0 %collective-permute-start = (bf16[576,144]{0,1:T(8,128)(2,1)}, bf16[576,144]{0,1:T(8,128)(2,1)}, u32[]{:S(2)}, u32[]{:S(2)}) collective-permute-start(bf16[576,144]{0,1:T(8,128)(2,1)} %get-tuple-element.28), channel_id=1, source_target_pairs={{0,2},{2,4},{4,6},{6,8},{8,10},{10,12},{12,14},{14,0},{1,3},{3,5},... | collective-permute-start | bytes 497672 | tf_op jit(solution)/shard_map/ppermute | solution.py:21
  15.8 2.3 copy-start.11
  15.8 1.2 copy-start
  21.5 94.4 %collective-permute-start.8 = (bf16[576,144]{0,1:T(8,128)(2,1)}, bf16[576,144]{0,1:T(8,128)(2,1)}, u32[]{:S(2)}, u32[]{:S(2)}) collective-permute-start(bf16[576,144]{0,1:T(8,128)(2,1)} %collective-permute-done.7), channel_id=1, source_target_pairs={{0,2},{2,4},{4,6},{6,8},{8,10},{10,12},{12,14},{14,0},{1,3},{3,5},... | collective-permute-start | bytes 497672 | tf_op jit(solution)/shard_map/ppermute | solution.py:21
  24.8 93.1 %collective-permute-start.1 = (bf16[576,144]{0,1:T(8,128)(2,1)}, bf16[576,144]{0,1:T(8,128)(2,1)}, u32[]{:S(2)}, u32[]{:S(2)}) collective-permute-start(bf16[576,144]{0,1:T(8,128)(2,1)} %collective-permute-done), channel_id=1, source_target_pairs={{0,2},{2,4},{4,6},{6,8},{8,10},{10,12},{12,14},{14,0},{1,3},{3,5},... | collective-permute-start | bytes 497672 | tf_op jit(solution)/shard_map/ppermute | solution.py:21
  102.9 1.2 copy-start.8
  108.1 1.7 copy-start.5
  111.4 96.1 %all-to-all-start = ((bf16[3,8,16,10,72]{4,2,3,0,1:T(8,128)(2,1)}), bf16[3,8,16,10,72]{4,2,3,0,1:T(8,128)(2,1)S(1)}, u32[]{:S(2)}, u32[]{:S(2)}) async-start(bf16[3,8,16,10,72]{4,2,3,0,1:T(8,128)(2,1)} %copy.95), calls=%async_computation | async-start | bytes 1966080 | tf_op jit(solution)/shard_map/all_to_all | solution.py:81
  115.9 33.6 %collective-permute-start.9 = (bf16[576,144]{0,1:T(8,128)(2,1)}, bf16[576,144]{0,1:T(8,128)(2,1)S(1)}, u32[]{:S(2)}, u32[]{:S(2)}) collective-permute-start(bf16[576,144]{0,1:T(8,128)(2,1)} %collective-permute-done.8), channel_id=1, source_target_pairs={{0,2},{2,4},{4,6},{6,8},{8,10},{10,12},{12,14},{14,0},{1,3},{3,5},... | collective-permute-start | bytes 497672 | tf_op jit(solution)/shard_map/ppermute | solution.py:21
  117.9 39.5 %collective-permute-start.2 = (bf16[576,144]{0,1:T(8,128)(2,1)}, bf16[576,144]{0,1:T(8,128)(2,1)S(1)}, u32[]{:S(2)}, u32[]{:S(2)}) collective-permute-start(bf16[576,144]{0,1:T(8,128)(2,1)} %collective-permute-done.1), channel_id=1, source_target_pairs={{0,2},{2,4},{4,6},{6,8},{8,10},{10,12},{12,14},{14,0},{1,3},{3,5},... | collective-permute-start | bytes 497672 | tf_op jit(solution)/shard_map/ppermute | solution.py:21
  149.5 15.9 %collective-permute-start.10 = (bf16[576,144]{0,1:T(8,128)(2,1)S(1)}, bf16[576,144]{0,1:T(8,128)(2,1)S(1)}, u32[]{:S(2)}, u32[]{:S(2)}) collective-permute-start(bf16[576,144]{0,1:T(8,128)(2,1)S(1)} %collective-permute-done.9), channel_id=1, source_target_pairs={{0,2},{2,4},{4,6},{6,8},{8,10},{10,12},{12,14},{14,0},{1,3},{3,5},... | collective-permute-start | bytes 497672 | tf_op jit(solution)/shard_map/ppermute | solution.py:21
  157.4 15.8 %collective-permute-start.3 = (bf16[576,144]{0,1:T(8,128)(2,1)S(1)}, bf16[576,144]{0,1:T(8,128)(2,1)S(1)}, u32[]{:S(2)}, u32[]{:S(2)}) collective-permute-start(bf16[576,144]{0,1:T(8,128)(2,1)S(1)} %collective-permute-done.2), channel_id=1, source_target_pairs={{0,2},{2,4},{4,6},{6,8},{8,10},{10,12},{12,14},{14,0},{1,3},{3,5},... | collective-permute-start | bytes 497672 | tf_op jit(solution)/shard_map/ppermute | solution.py:21
  165.4 15.8 %collective-permute-start.11 = (bf16[576,144]{0,1:T(8,128)(2,1)S(1)}, bf16[576,144]{0,1:T(8,128)(2,1)S(1)}, u32[]{:S(2)}, u32[]{:S(2)}) collective-permute-start(bf16[576,144]{0,1:T(8,128)(2,1)S(1)} %collective-permute-done.10), channel_id=1, source_target_pairs={{0,2},{2,4},{4,6},{6,8},{8,10},{10,12},{12,14},{14,0},{1,3},{3,5},... | collective-permute-start | bytes 497672 | tf_op jit(solution)/shard_map/ppermute | solution.py:21
  173.2 15.8 %collective-permute-start.4 = (bf16[576,144]{0,1:T(8,128)(2,1)S(1)}, bf16[576,144]{0,1:T(8,128)(2,1)S(1)}, u32[]{:S(2)}, u32[]{:S(2)}) collective-permute-start(bf16[576,144]{0,1:T(8,128)(2,1)S(1)} %collective-permute-done.3), channel_id=1, source_target_pairs={{0,2},{2,4},{4,6},{6,8},{8,10},{10,12},{12,14},{14,0},{1,3},{3,5},... | collective-permute-start | bytes 497672 | tf_op jit(solution)/shard_map/ppermute | solution.py:21
  181.2 15.7 %collective-permute-start.12 = (bf16[576,144]{0,1:T(8,128)(2,1)S(1)}, bf16[576,144]{0,1:T(8,128)(2,1)S(1)}, u32[]{:S(2)}, u32[]{:S(2)}) collective-permute-start(bf16[576,144]{0,1:T(8,128)(2,1)S(1)} %collective-permute-done.11), channel_id=1, source_target_pairs={{0,2},{2,4},{4,6},{6,8},{8,10},{10,12},{12,14},{14,0},{1,3},{3,5},... | collective-permute-start | bytes 497672 | tf_op jit(solution)/shard_map/ppermute | solution.py:21
  189.0 15.8 %collective-permute-start.5 = (bf16[576,144]{0,1:T(8,128)(2,1)S(1)}, bf16[576,144]{0,1:T(8,128)(2,1)S(1)}, u32[]{:S(2)}, u32[]{:S(2)}) collective-permute-start(bf16[576,144]{0,1:T(8,128)(2,1)S(1)} %collective-permute-done.4), channel_id=1, source_target_pairs={{0,2},{2,4},{4,6},{6,8},{8,10},{10,12},{12,14},{14,0},{1,3},{3,5},... | collective-permute-start | bytes 497672 | tf_op jit(solution)/shard_map/ppermute | solution.py:21
  196.9 17.8 %collective-permute-start.13 = (bf16[576,144]{0,1:T(8,128)(2,1)S(1)}, bf16[576,144]{0,1:T(8,128)(2,1)S(1)}, u32[]{:S(2)}, u32[]{:S(2)}) collective-permute-start(bf16[576,144]{0,1:T(8,128)(2,1)S(1)} %collective-permute-done.12), channel_id=1, source_target_pairs={{0,2},{2,4},{4,6},{6,8},{8,10},{10,12},{12,14},{14,0},{1,3},{3,5},... | collective-permute-start | bytes 497672 | tf_op jit(solution)/shard_map/ppermute | solution.py:21
  204.8 9.9 %collective-permute-start.6 = (bf16[576,144]{0,1:T(8,128)(2,1)S(1)}, bf16[576,144]{0,1:T(8,128)(2,1)}, u32[]{:S(2)}, u32[]{:S(2)}) collective-permute-start(bf16[576,144]{0,1:T(8,128)(2,1)S(1)} %collective-permute-done.5), channel_id=1, source_target_pairs={{0,2},{2,4},{4,6},{6,8},{8,10},{10,12},{12,14},{14,0},{1,3},{3,5},... | collective-permute-start | bytes 497672 | tf_op jit(solution)/shard_map/ppermute | solution.py:21
  209.4 14.3 %all-to-all-start.1 = ((bf16[1,16,80,72]{3,1,0,2:T(8,128)(2,1)}), bf16[1,16,80,72]{3,1,0,2:T(8,128)(2,1)S(1)}, u32[]{:S(2)}, u32[]{:S(2)}) async-start(bf16[1,16,80,72]{3,1,0,2:T(8,128)(2,1)} %copy.100), calls=%async_computation.1 | async-start | bytes 655360 | tf_op jit(solution)/shard_map/all_to_all | solution.py:83
  214.7 9.4 %copy-start.3 = (f32[160,1152]{1,0:T(8,128)S(1)}, f32[160,1152]{1,0:T(8,128)}, u32[]{:S(2)}) copy-start(f32[160,1152]{1,0:T(8,128)} %reshape.226) | copy-start | bytes 2211844
  241.3 1.0 copy-start.6
  241.3 1.2 copy-start.7
  250.0 4.8 %copy-start.1 = (bf16[576,1152]{0,1:T(8,128)(2,1)S(1)}, bf16[576,1152]{0,1:T(8,128)(2,1)}, u32[]{:S(2)}) copy-start(bf16[576,1152]{0,1:T(8,128)(2,1)} %get-tuple-element.49) | copy-start | bytes 3981316
Sparse Core Ops, SparseCore 0:
  9.6 83.0 all-gather.4
  94.9 95.0 all-gather.6
